TPU v7x, 32 devices: a whole 2x2x4 slice. The times are simulated.
32 devices in a mesh: bins: 4 (over y, x), batch: 4 (over z), fsdp: 2 (over core).
Axes of the slice: x: 2, y: 2, z: 4, core: 2. Of those that a mesh axis runs over, the one named last changes fastest.
Arguments:
- track_in: bfloat16 [64, 1024, 768], P(('batch', 'fsdp'), 'bins'), may hold values from -6 to 6
- black_mask: int32 [64, 1024], P(('batch', 'fsdp'), 'bins'), may hold values 0 or 1
- unmap_mask: int32 [64, 1024], P(('batch', 'fsdp'), 'bins'), may hold values 0 or 1
- seq_valid: int32 [64], P(('batch', 'fsdp')), may hold values from 256 to 1024
- dilated_weight: float32 [2304, 384], P(('batch', 'fsdp')), may hold values from -0.125 to 0.125
- point_weight: float32 [384, 768], P(('batch', 'fsdp')), may hold values from -0.30618622 to 0.30618622
- point_bias: float32 [768], P(('batch', 'fsdp')), may hold values from -3 to 3
- gain_first: float32 [768], P(('batch', 'fsdp')), may hold values from 0.5 to 2
- shift_first: float32 [768], P(('batch', 'fsdp')), may hold values from -3 to 3
- gain_second: float32 [384], P(('batch', 'fsdp')), may hold values from 0.5 to 2
- shift_second: float32 [384], P(('batch', 'fsdp')), may hold values from -3 to 3
- out_grad: bfloat16 [64, 1024, 768], P(('batch', 'fsdp'), 'bins'), may hold values from -8 to 8
Outputs:
- block_out: bfloat16 [64, 1024, 768], P(('batch', 'fsdp'), 'bins')
- input_grad: bfloat16 [64, 1024, 768], P(('batch', 'fsdp'), 'bins')
- dilated_grad: float32 [2304, 384], P(('batch', 'fsdp'))
- point_grad: float32 [384, 768], P(('batch', 'fsdp'))
- bias_grad: float32 [768], P(('batch', 'fsdp'))
- gain_first_grad: float32 [768], P(('batch', 'fsdp'))
- shift_first_grad: float32 [768], P(('batch', 'fsdp'))
- gain_second_grad: float32 [384], P(('batch', 'fsdp'))
- shift_second_grad: float32 [384], P(('batch', 'fsdp'))
All inputs are finite; a program needn't handle non-finite values. No bound on the sum of `black_mask` or of `unmap_mask` on one device may be relied on, other than what follows from the above.
Results may differ from a plain program's by a relative error of at most 0.0074.
Values may be sent and summed in bfloat16 or wider, within the bound.
A program may use at most 128 MiB of HBM per device.

v0:
```python
import jax
import jax.numpy as jnp
from jax import lax
from jax.sharding import PartitionSpec as P

DILATION_STEP = 26
norm_eps = 1e-05


def extended(block, sides, width):
    for axis, dim in sides:
        count = lax.axis_size(axis)
        forward = [(i, i + 1) for i in range(count - 1)]
        backward = [(target, source) for source, target in forward]
        low = lax.ppermute(
            lax.slice_in_dim(block, block.shape[dim] - width, None, axis=dim), axis, forward
        )
        high = lax.ppermute(lax.slice_in_dim(block, 0, width, axis=dim), axis, backward)
        block = jnp.concatenate([low, block, high], axis=dim)
    return block


def activate(values):
    return values * jax.nn.sigmoid(1.702 * values)


def slope(values):
    sigma = jax.nn.sigmoid(1.702 * values)
    return sigma + 1.702 * values * sigma * (1.0 - sigma)


def moments(values, valid, local_count):
    total, count = lax.psum(
        (jnp.sum(values * valid, axis=0), local_count), ("bins", "batch", "fsdp")
    )
    mean = total / count
    centred = values - mean
    spread = lax.psum(jnp.sum(centred * centred * valid, axis=0), ("bins", "batch", "fsdp"))
    variance = spread / count
    scale = lax.rsqrt(variance + norm_eps)
    return (centred * scale, scale, count)


def norm_back(grad_out, normed, scale, gain, valid, count):
    total, cross = lax.psum(
        (jnp.sum(grad_out, axis=0), jnp.sum(grad_out * normed, axis=0)), ("bins", "batch", "fsdp")
    )
    grad_in = scale * gain * (grad_out - valid * (total + normed * cross) / count)
    return (grad_in, total, cross)


def contract_rows(left, right):
    return lax.dot_general(
        left, right, (((0,), (0,)), ((), ())), preferred_element_type=jnp.float32
    )


def local(
    track_in,
    black_mask,
    unmap_mask,
    seq_valid,
    dilated_weight,
    point_weight,
    point_bias,
    gain_first,
    shift_first,
    gain_second,
    shift_second,
    out_grad,
):
    sequence_count, count_of_bins, channel_count = track_in.shape
    row_count = sequence_count * count_of_bins
    bf = jnp.bfloat16
    gathered_taps = (
        lax.all_gather(dilated_weight.astype(bf), ("batch", "fsdp"), axis=0, tiled=True),
        lax.all_gather(point_weight.astype(bf), ("batch", "fsdp"), axis=0, tiled=True),
        lax.all_gather(point_bias.astype(bf), ("batch", "fsdp"), axis=0, tiled=True),
        lax.all_gather(gain_first.astype(bf), ("batch", "fsdp"), axis=0, tiled=True),
        lax.all_gather(shift_first.astype(bf), ("batch", "fsdp"), axis=0, tiled=True),
        lax.all_gather(gain_second.astype(bf), ("batch", "fsdp"), axis=0, tiled=True),
        lax.all_gather(shift_second.astype(bf), ("batch", "fsdp"), axis=0, tiled=True),
    )
    dilation_weight = gathered_taps[0]
    pointwise_weight = gathered_taps[1]
    hidden_state = pointwise_weight.shape[0]
    bias_vector = gathered_taps[2].astype(jnp.float32)
    first_gain = gathered_taps[3].astype(jnp.float32)
    first_offset = gathered_taps[4].astype(jnp.float32)
    second_gain = gathered_taps[5].astype(jnp.float32)
    second_offset = gathered_taps[6].astype(jnp.float32)
    place = lax.axis_index("bins") * count_of_bins + lax.broadcasted_iota(
        jnp.int32, (sequence_count, count_of_bins), 1
    )
    keep = (black_mask == 0) & (unmap_mask == 0) & (place < seq_valid[:, None])
    valid = keep.astype(jnp.float32).reshape(row_count, 1)
    local_count = jnp.sum(valid)
    input_signal = track_in.reshape(row_count, channel_count).astype(jnp.float32)
    normed_one, scale_one, count = moments(input_signal, valid, local_count)
    pre_one = normed_one * first_gain + first_offset
    first_hidden = activate(pre_one).astype(bf)
    first_padded = extended(
        first_hidden.reshape(sequence_count, count_of_bins, channel_count),
        (("bins", 1),),
        DILATION_STEP,
    )
    kernel_taps = jnp.concatenate(
        [
            first_padded[
                :,
                kernel_tap_index * DILATION_STEP : kernel_tap_index * DILATION_STEP + count_of_bins,
                :,
            ]
            for kernel_tap_index in range(3)
        ],
        axis=2,
    ).reshape(row_count, 3 * channel_count)
    convolution_output = jnp.dot(kernel_taps, dilation_weight, preferred_element_type=jnp.float32)
    normed_two, scale_two, count_again = moments(convolution_output, valid, local_count)
    pre_two = normed_two * second_gain + second_offset
    hidden_two = activate(pre_two).astype(bf)
    branch = jnp.dot(hidden_two, pointwise_weight, preferred_element_type=jnp.float32)
    block_out = (
        (input_signal + branch + bias_vector)
        .astype(bf)
        .reshape(sequence_count, count_of_bins, channel_count)
    )
    grad = out_grad.reshape(row_count, channel_count) * keep.reshape(row_count, 1).astype(bf)
    point_local = contract_rows(hidden_two, grad)
    bias_local = jnp.sum(grad, axis=0, dtype=jnp.float32)
    grad_two = jnp.dot(grad, pointwise_weight.T, preferred_element_type=jnp.float32) * slope(
        pre_two
    )
    convolution_gradient, shift_two_total, gain_two_total = norm_back(
        grad_two, normed_two, scale_two, second_gain, valid, count
    )
    convolution_gradient = convolution_gradient.astype(bf)
    dilated_local = contract_rows(kernel_taps, convolution_gradient)
    padded_gradient = extended(
        convolution_gradient.reshape(sequence_count, count_of_bins, hidden_state),
        (("bins", 1),),
        DILATION_STEP,
    )
    back_taps = jnp.concatenate(
        [
            padded_gradient[
                :,
                (2 - kernel_tap_index) * DILATION_STEP : (2 - kernel_tap_index) * DILATION_STEP
                + count_of_bins,
                :,
            ]
            for kernel_tap_index in range(3)
        ],
        axis=2,
    ).reshape(row_count, 3 * hidden_state)
    weight_backward = jnp.transpose(
        dilation_weight.reshape(3, channel_count, hidden_state), (0, 2, 1)
    ).reshape(3 * hidden_state, channel_count)
    grad_one = jnp.dot(back_taps, weight_backward, preferred_element_type=jnp.float32) * slope(
        pre_one
    )
    input_part, shift_one_total, gain_one_total = norm_back(
        grad_one, normed_one, scale_one, first_gain, valid, count
    )
    input_grad = (
        (grad.astype(jnp.float32) + input_part)
        .astype(bf)
        .reshape(sequence_count, count_of_bins, channel_count)
    )
    local_grads = (dilated_local, point_local, bias_local)
    summed = lax.psum((local_grads[0], local_grads[1], local_grads[2]), "bins")
    shares = (
        lax.psum_scatter(summed[0], ("batch", "fsdp"), scatter_dimension=0, tiled=True),
        lax.psum_scatter(summed[1], ("batch", "fsdp"), scatter_dimension=0, tiled=True),
        lax.psum_scatter(summed[2], ("batch", "fsdp"), scatter_dimension=0, tiled=True),
    )
    owner = lax.axis_index(("batch", "fsdp"))
    group_size = lax.axis_size(("batch", "fsdp"))
    wide_share = channel_count // group_size
    narrow_share = hidden_state // group_size
    gain_first_grad = lax.dynamic_slice_in_dim(gain_one_total, owner * wide_share, wide_share)
    shift_first_grad = lax.dynamic_slice_in_dim(shift_one_total, owner * wide_share, wide_share)
    gain_second_grad = lax.dynamic_slice_in_dim(gain_two_total, owner * narrow_share, narrow_share)
    shift_second_grad = lax.dynamic_slice_in_dim(
        shift_two_total, owner * narrow_share, narrow_share
    )
    return (
        block_out,
        input_grad,
        shares[0],
        shares[1],
        shares[2],
        gain_first_grad,
        shift_first_grad,
        gain_second_grad,
        shift_second_grad,
    )


def solution(mesh):
    return jax.shard_map(
        local,
        mesh=mesh,
        in_specs=(
            P(("batch", "fsdp"), "bins", None),
            P(("batch", "fsdp"), "bins"),
            P(("batch", "fsdp"), "bins"),
            P(("batch", "fsdp")),
            P(("batch", "fsdp"), None),
            P(("batch", "fsdp"), None),
            P(("batch", "fsdp")),
            P(("batch", "fsdp")),
            P(("batch", "fsdp")),
            P(("batch", "fsdp")),
            P(("batch", "fsdp")),
            P(("batch", "fsdp"), "bins", None),
        ),
        out_specs=(
            P(("batch", "fsdp"), "bins", None),
            P(("batch", "fsdp"), "bins", None),
            P(("batch", "fsdp"), None),
            P(("batch", "fsdp"), None),
            P(("batch", "fsdp")),
            P(("batch", "fsdp")),
            P(("batch", "fsdp")),
            P(("batch", "fsdp")),
            P(("batch", "fsdp")),
        ),
        check_vma=False,
    )
```

profile of v0, /device:TPU:0, one launch (start us, length us, event | category | flops | bytes accessed | tf_op | source)
XLA Modules:
  0.0 466.3 jit_solution(5711937940642805629)
XLA Ops:
  7.2 1.9 convert_element_type.96
  17.6 19.0 %all-reduce.10 = (bf16[768]{0:T(1024)(128)(2,1)S(1)}, bf16[768]{0:T(1024)(128)(2,1)S(1)}, bf16[768]{0:T(1024)(128)(2,1)S(1)}, bf16[384]{0:T(512)(128)(2,1)S(1)}, bf16[384]{0:T(512)(128)(2,1)S(1)}) all-reduce(bf16[768]{0:T(1024)(128)(2,1)S(1)} %dynamic-update-slice.4, ...), channel_id=1, replica_groups=mesh['bins'=4,'batch'=4,'fsdp'=2] {'batch','fsdp'}, use_global_device_ids=true, to_apply=%add.4 | all-reduce | flops 3072 | bytes 12288
  36.7 2.6 fusion.13
  39.3 38.0 %all-reduce.8 = (f32[768]{0:T(1024)S(1)}, f32[]{:T(128)}) all-reduce(f32[768]{0:T(1024)S(1)} %fusion.13, f32[]{:T(128)} %convert_reduce_fusion.1), channel_id=1, replica_groups=mesh['bins'=4,'batch'=4,'fsdp'=2] {'bins','batch','fsdp'}, use_global_device_ids=true, to_apply=%region_1.0 | all-reduce | flops 769 | bytes 6152 | tf_op jit(solution)/shard_map/psum | solution.py:33
  79.0 41.7 %psum.89 = f32[768]{0:T(1024)S(1)} all-reduce(f32[768]{0:T(1024)S(1)} %fusion.3), channel_id=1, replica_groups=mesh['bins'=4,'batch'=4,'fsdp'=2] {'bins','batch','fsdp'}, use_global_device_ids=true, to_apply=%region_5.0 | all-reduce | flops 768 | bytes 6144 | tf_op jit(solution)/shard_map/psum | solution.py:38
  121.9 2.4 fusion.12
  124.5 4.2 collective-permute-start
  130.0 2.3 bitcast_multiply_fusion
  132.3 15.8 %all_gather.26 = bf16[384,768]{1,0:T(8,128)(2,1)} all-gather(bf16[48,768]{1,0:T(8,128)(2,1)S(1)} %convert_element_type.102), channel_id=1, replica_groups=mesh['bins'=4,'batch'=4,'fsdp'=2] {'batch','fsdp'}, dimensions={0}, use_global_device_ids=true | all-gather | bytes 663552 | tf_op jit(solution)/shard_map/all_gather | solution.py:77
  148.2 3.6 pad_maximum_fusion.4
  151.8 9.3 %multiply_reduce_fusion.2 = (f32[384]{0:T(512)S(1)}, f32[2048,384]{1,0:T(8,128)}) fusion(f32[2048]{0:T(1024)S(1)} %bitcast.82, bf16[2304,384]{1,0:T(8,128)(2,1)} %all-gather.2.cloned.1.call-done, bf16[2048,768]{1,0:T(8,128)(2,1)} %bitcast.75, bf16[2048,768]{1,0:T(8,128)(2,1)} %bitcast.69, bf16[2048,768]{1,0:T(8,128)(2,1)} %bitcast.73), kind=kOutput, calls=%fused_computation.55 | convolution fusion | flops 3653762560 | bytes 14362112 | tf_op jit(solution)/shard_map/dot_general | solution.py:118
  161.0 39.7 %psum.90 = f32[384]{0:T(512)S(1)} all-reduce(f32[384]{0:T(512)S(1)} %get-tuple-element.45), channel_id=1, replica_groups=mesh['bins'=4,'batch'=4,'fsdp'=2] {'bins','batch','fsdp'}, use_global_device_ids=true, to_apply=%region_7.0 | all-reduce | flops 384 | bytes 3072 | tf_op jit(solution)/shard_map/psum | solution.py:33
  201.4 2.3 multiply_reduce_fusion.1
  203.7 41.8 %psum.91 = f32[384]{0:T(512)S(1)} all-reduce(f32[384]{0:T(512)S(1)} %multiply_reduce_fusion.1), channel_id=1, replica_groups=mesh['bins'=4,'batch'=4,'fsdp'=2] {'bins','batch','fsdp'}, use_global_device_ids=true, to_apply=%region_9.0 | all-reduce | flops 384 | bytes 3072 | tf_op jit(solution)/shard_map/psum | solution.py:38
  246.2 5.5 %fusion.43 = f32[384,768]{1,0:T(8,128)} fusion(bf16[2048,768]{1,0:T(8,128)(2,1)} %bitcast_multiply_fusion, f32[2048,384]{1,0:T(8,128)} %get-tuple-element.46, f32[384]{0:T(512)S(1)} %convert_element_type.100, f32[384]{0:T(512)S(1)} %convert_element_type.98, f32[384]{0:T(512)S(1)} %get-tuple-element.31, f32[384]{0:T(512)S(1)} %broadcast_divide_fusion.1), kind=kOutput, calls=%fused_computation.73 | convolution fusion | flops 1215823872 | bytes 7477248 | tf_op jit(solution)/shard_map/dot_general | solution.py:53
  251.8 7.8 %fusion.45 = (f32[384]{0:T(512)S(1)}, f32[384]{0:T(512)S(1)}, f32[2048,384]{1,0:T(8,128)}) fusion(f32[384]{0:T(512)S(1)} %get-tuple-element.31, f32[2048,384]{1,0:T(8,128)} %get-tuple-element.46, f32[384]{0:T(512)S(1)} %broadcast_divide_fusion.1, f32[384]{0:T(512)S(1)} %convert_element_type.100, f32[384]{0:T(512)S(1)} %convert_element_type.98, ...), kind=kOutput, calls=%fused_computation.75 | convolution fusion | flops 1220541696 | bytes 10036224 | tf_op jit(solution)/shard_map/dot_general | solution.py:131
  259.6 38.6 %all-reduce.7 = (f32[384]{0:T(512)S(1)}, f32[384]{0:T(512)S(1)}) all-reduce(f32[384]{0:T(512)S(1)} %get-tuple-element.12, f32[384]{0:T(512)S(1)} %get-tuple-element.11), channel_id=1, replica_groups=mesh['bins'=4,'batch'=4,'fsdp'=2] {'bins','batch','fsdp'}, use_global_device_ids=true, to_apply=%region_13.0 | all-reduce | flops 768 | bytes 6144 | tf_op jit(solution)/shard_map/psum | solution.py:45
  298.3 4.5 multiply_convert_fusion
  303.9 6.8 %fusion.36 = f32[2304,384]{1,0:T(8,128)} fusion(bf16[2048,384]{1,0:T(8,128)(2,1)S(1)} %multiply_convert_fusion, bf16[2048,768]{1,0:T(8,128)(2,1)} %bitcast.76, bf16[2048,768]{1,0:T(8,128)(2,1)S(1)} %bitcast.70, bf16[2048,768]{1,0:T(8,128)(2,1)S(1)} %bitcast.74), kind=kOutput, calls=%fused_computation.43 | convolution fusion | flops 3652190208 | bytes 14548992 | tf_op jit(solution)/shard_map/dot_general | solution.py:53
  312.1 2.6 convert_reduce_fusion
  314.6 14.9 %all-reduce.5 = f32[768]{0:T(1024)S(1)} all-reduce(f32[768]{0:T(1024)S(1)} %convert_reduce_fusion), channel_id=4, replica_groups=mesh['bins'=4,'batch'=4,'fsdp'=2] {'batch','fsdp'}, use_global_device_ids=true, to_apply=%region_24.0.clone | all-reduce | flops 768 | bytes 6144
  329.6 10.6 %psum.101 = f32[96]{0:T(128)} all-reduce(f32[96]{0:T(128)S(1)} %dynamic-slice.6), channel_id=1, replica_groups=mesh['bins'=4,'batch'=4,'fsdp'=2] {'bins'}, use_global_device_ids=true, to_apply=%region_23.0 | all-reduce | flops 96 | bytes 768 | tf_op jit(solution)/shard_map/psum | solution.py:171
  340.2 1.8 fusion.48
  343.3 4.8 %collective-permute-start.3 = (bf16[8,26,384]{2,1,0:T(8,128)(2,1)}, bf16[8,26,384]{2,1,0:T(8,128)(2,1)S(1)}, u32[]{:S(2)}, u32[]{:S(2)}) collective-permute-start(bf16[8,26,384]{2,1,0:T(8,128)(2,1)} %get-tuple-element.39), channel_id=1, source_target_pairs={{0,8},{8,16},{16,24},{1,9},{9,17},{17,25},{2,10},{10,18},{18,26},{... | collective-permute-start | bytes 479240 | tf_op jit(solution)/shard_map/ppermute | solution.py:15
  348.1 6.4 %fusion.15 = bf16[2048,768]{1,0:T(8,128)(2,1)} fusion(bf16[8,256,768]{2,1,0:T(8,128)(2,1)S(1)} %copy-done, bf16[384,768]{1,0:T(8,128)(2,1)} %all_gather.26, f32[768]{0:T(1024)} %convert_element_type.104, f32[2048,384]{1,0:T(8,128)} %get-tuple-element.46, f32[384]{0:T(512)} %copy-done.20, f32[384]{0:T(512)} %copy-done.21, f32[384]{0:T(512)} %copy-done.17, ...), kind=kOutput, calls=%fused_computation.20 | convolution fusion | flops 1222115328 | bytes 10036224 | tf_op jit(solution)/shard_map/dot_general | solution.py:122
  356.9 3.8 copy.22
  360.8 3.1 pad_maximum_fusion.6
  364.0 8.4 %fusion.44 = (f32[768]{0:T(1024)S(1)}, f32[768]{0:T(1024)S(1)}, f32[2048,768]{1,0:T(8,128)}) fusion(f32[768]{0:T(1024)S(1)} %get-tuple-element.29, f32[768]{0:T(1024)S(1)} %broadcast_divide_fusion, bf16[8,256,768]{2,1,0:T(8,128)(2,1)S(1)} %copy-done, f32[768]{0:T(1024)S(1)} %copy-done.13, f32[768]{0:T(1024)S(1)} %copy-done.15, ...), kind=kOutput, calls=%fused_computation.74 | convolution fusion | flops 3664771584 | bytes 15943680 | tf_op jit(solution)/shard_map/dot_general | solution.py:159
  372.3 37.0 %all-reduce.6 = (f32[768]{0:T(1024)S(1)}, f32[768]{0:T(1024)S(1)}) all-reduce(f32[768]{0:T(1024)S(1)} %get-tuple-element.10, f32[768]{0:T(1024)S(1)} %get-tuple-element.9), channel_id=1, replica_groups=mesh['bins'=4,'batch'=4,'fsdp'=2] {'bins','batch','fsdp'}, use_global_device_ids=true, to_apply=%region_17.0 | all-reduce | flops 1536 | bytes 12288 | tf_op jit(solution)/shard_map/psum | solution.py:45
  409.4 6.9 %fusion.29 = bf16[2048,768]{1,0:T(8,128)(2,1)} fusion(f32[2048,768]{1,0:T(8,128)} %get-tuple-element.48, bf16[8,256,768]{2,1,0:T(8,128)(2,1)S(1)} %copy-done, f32[]{:T(128)} %get-tuple-element.18, f32[768]{0:T(1024)S(1)} %get-tuple-element.13, f32[768]{0:T(1024)S(1)} %get-tuple-element.14, f32[2048]{0:T(1024)S(1)} %bitcast.85, ...), kind=kLoop, calls=%fused_computation.36 | loop fusion | flops 20447232 | bytes 15756292 | tf_op jit(solution)/shard_map/convert_element_type | solution.py:167
  417.4 39.0 %all-reduce.13.cloned.1.call-done = (f32[288,384]{1,0:T(8,128)}, f32[48,768]{1,0:T(8,128)}) async-done(((f32[288,384]{1,0:T(8,128)}, f32[48,768]{1,0:T(8,128)}), (f32[288,384]{1,0:T(8,128)}, f32[48,768]{1,0:T(8,128)})) %all-reduce.13.cloned.1.call-update) | async-done | bytes 589840 | tf_op jit(solution)/shard_map/psum | solution.py:171
  456.4 1.8 copy.32
  (101 shorter events, 21.3 us)
Async XLA Ops:
  7.2 70.7 %copy-start = (bf16[8,256,768]{2,1,0:T(8,128)(2,1)S(1)}, bf16[8,256,768]{2,1,0:T(8,128)(2,1)}, u32[]{:S(2)}) copy-start(bf16[8,256,768]{2,1,0:T(8,128)(2,1)} %param.12) | copy-start | bytes 9437188
  7.2 144.6 %all-gather.2.cloned.1.call-start = ((), (), s32[]{:S(2)}) async-start(), calls=%async_computation.2 | async-start | bytes 1990656 | tf_op jit(solution)/shard_map/all_gather | solution.py:76
  9.1 400.2 %reduce-scatter.5.cloned.1.call-start = ((), (), s32[]{:S(2)}) async-start(), calls=%async_computation.4 | async-start | bytes 1327104 | tf_op jit(solution)/shard_map/reduce_scatter | solution.py:174
  36.6 85.3 %copy-start.12 = (f32[768]{0:T(1024)}, f32[768]{0:T(1024)S(1)}, u32[]{:S(2)}) copy-start(f32[768]{0:T(1024)S(1)} %convert_element_type.94) | copy-start | bytes 9220
  36.6 85.3 %copy-start.14 = (f32[768]{0:T(1024)}, f32[768]{0:T(1024)S(1)}, u32[]{:S(2)}) copy-start(f32[768]{0:T(1024)S(1)} %convert_element_type.92) | copy-start | bytes 9220
  121.9 8.1 %copy-start.1 = (bf16[8,256,768]{2,1,0:T(8,128)(2,1)S(1)}, bf16[8,256,768]{2,1,0:T(8,128)(2,1)}, u32[]{:S(2)}) copy-start(bf16[8,256,768]{2,1,0:T(8,128)(2,1)} %param.23) | copy-start | bytes 9437188
  124.3 23.8 %copy-start.2 = (bf16[8,256,768]{2,1,0:T(8,128)(2,1)}, bf16[8,256,768]{2,1,0:T(8,128)(2,1)S(1)}, u32[]{:S(2)}) copy-start(bf16[8,256,768]{2,1,0:T(8,128)(2,1)S(1)} %fusion.12) | copy-start | bytes 9437188
  124.5 23.7 %collective-permute-start = (bf16[8,26,768]{2,1,0:T(8,128)(2,1)S(1)}, bf16[8,26,768]{2,1,0:T(8,128)(2,1)S(1)}, u32[]{:S(2)}, u32[]{:S(2)}) collective-permute-start(bf16[8,26,768]{2,1,0:T(8,128)(2,1)S(1)} %get-tuple-element.34), channel_id=1, source_target_pairs={{0,8},{8,16},{16,24},{1,9},{9,17},{17,25},{2,10},{10,18},{18,26},{... | collective-permute-start | bytes 958472 | tf_op jit(solution)/shard_map/ppermute | solution.py:15
  128.7 19.5 %collective-permute-start.1 = (bf16[8,26,768]{2,1,0:T(8,128)(2,1)S(1)}, bf16[8,26,768]{2,1,0:T(8,128)(2,1)S(1)}, u32[]{:S(2)}, u32[]{:S(2)}) collective-permute-start(bf16[8,26,768]{2,1,0:T(8,128)(2,1)S(1)} %get-tuple-element.35), channel_id=1, source_target_pairs={{8,0},{16,8},{24,16},{9,1},{17,9},{25,17},{10,2},{18,10},{26,18},{... | collective-permute-start | bytes 958472 | tf_op jit(solution)/shard_map/ppermute | solution.py:18
  130.0 2.3 copy-start.9
  130.0 2.3 copy-start.8
  132.3 119.5 %copy-start.20 = (f32[384]{0:T(512)}, f32[384]{0:T(512)S(1)}, u32[]{:S(2)}) copy-start(f32[384]{0:T(512)S(1)} %convert_element_type.100) | copy-start | bytes 4612
  132.3 119.5 %copy-start.21 = (f32[384]{0:T(512)}, f32[384]{0:T(512)S(1)}, u32[]{:S(2)}) copy-start(f32[384]{0:T(512)S(1)} %convert_element_type.98) | copy-start | bytes 4612
  201.4 96.8 %copy-start.11 = (f32[384]{0:T(512)}, f32[384]{0:T(512)S(1)}, u32[]{:S(2)}) copy-start(f32[384]{0:T(512)S(1)} %broadcast_divide_fusion.1) | copy-start | bytes 4612
  246.2 52.0 %copy-start.17 = (f32[384]{0:T(512)}, f32[384]{0:T(512)S(1)}, u32[]{:S(2)}) copy-start(f32[384]{0:T(512)S(1)} %get-tuple-element.31) | copy-start | bytes 4612
  251.7 157.6 %reduce-scatter.3.cloned.1.call-start = ((), (), s32[]{:S(2)}) async-start(), calls=%async_computation.3 | async-start | bytes 3981312 | tf_op jit(solution)/shard_map/reduce_scatter | solution.py:173
  298.2 4.6 copy-start.18
  298.2 4.6 copy-start.19
  298.2 5.7 %copy-start.3 = (bf16[8,256,768]{2,1,0:T(8,128)(2,1)S(1)}, bf16[8,256,768]{2,1,0:T(8,128)(2,1)}, u32[]{:S(2)}) copy-start(bf16[8,256,768]{2,1,0:T(8,128)(2,1)} %copy-done.2) | copy-start | bytes 9437188
  298.2 5.7 %copy-start.6 = (bf16[8,256,768]{2,1,0:T(8,128)(2,1)S(1)}, bf16[8,256,768]{2,1,0:T(8,128)(2,1)}, u32[]{:S(2)}) copy-start(bf16[8,256,768]{2,1,0:T(8,128)(2,1)} %get-tuple-element.32) | copy-start | bytes 9437188
  302.8 1.1 copy-start.4
  310.7 145.6 %all-reduce.13.cloned.1.call-start = ((), (), s32[]{:S(2)}) async-start(), calls=%async_computation.5 | async-start | bytes 1179648 | tf_op jit(solution)/shard_map/psum | solution.py:171
  342.0 18.8 %collective-permute-start.2 = (bf16[8,26,384]{2,1,0:T(8,128)(2,1)}, bf16[8,26,384]{2,1,0:T(8,128)(2,1)S(1)}, u32[]{:S(2)}, u32[]{:S(2)}) collective-permute-start(bf16[8,26,384]{2,1,0:T(8,128)(2,1)} %get-tuple-element.38), channel_id=1, source_target_pairs={{8,0},{16,8},{24,16},{9,1},{17,9},{25,17},{10,2},{18,10},{26,18},{... | collective-permute-start | bytes 479240 | tf_op jit(solution)/shard_map/ppermute | solution.py:18
  343.3 17.5 %collective-permute-start.3 = (bf16[8,26,384]{2,1,0:T(8,128)(2,1)}, bf16[8,26,384]{2,1,0:T(8,128)(2,1)S(1)}, u32[]{:S(2)}, u32[]{:S(2)}) collective-permute-start(bf16[8,26,384]{2,1,0:T(8,128)(2,1)} %get-tuple-element.39), channel_id=1, source_target_pairs={{0,8},{8,16},{16,24},{1,9},{9,17},{17,25},{2,10},{10,18},{18,26},{... | collective-permute-start | bytes 479240 | tf_op jit(solution)/shard_map/ppermute | solution.py:15
  360.8 3.1 copy-start.5
  360.8 3.1 copy-start.7
  360.8 3.2 copy-start.13
  360.8 3.2 copy-start.15
  363.9 45.4 %copy-start.10 = (bf16[1,2,8,128]{3,1,2,0:T(2,128)(2,1)S(1)}, bf16[1,2,8,128]{3,1,2,0:T(2,128)(2,1)}, u32[]{:S(2)}) copy-start(bf16[1,2,8,128]{3,1,2,0:T(2,128)(2,1)} %copy-done.9) | copy-start | bytes 12292
  363.9 45.4 %copy-start.16 = (f32[768]{0:T(1024)S(1)}, f32[768]{0:T(1024)}, u32[]{:S(2)}) copy-start(f32[768]{0:T(1024)} %get-tuple-element.28) | copy-start | bytes 9220
Sparse Core Ops, SparseCore 0:
  10.2 29.7 all-gather.1
  251.9 31.9 reduce-scatter.4
  310.9 44.6 reduce-scatter.2
  409.5 46.8 all-reduce.12
where the time goes:
time: 468 us; the launch traced here: 466 us
  blocking collectives  297 us (63%)
  matrix products  44.1 us (9%)
  other arithmetic  41.7 us (9%)
  waiting for transfers between devices  39.1 us (8%)
  local copies, waits for them, and re-layouts  16.4 us (4%)
  between operations  16.2 us (3%)
  starting transfers between devices  11.7 us (2%)
    psum x2, blocking collectives, moments(): lax.psum(jnp.sum(centred * centred * valid, axis=0), ('bins', 'batch', 'f...  83.5 us
    psum x2, blocking collectives, moments(): lax.psum((jnp.sum(values * valid, axis=0), local_count), ('bins', 'batch'...  77.7 us
    psum x2, blocking collectives, norm_back(): lax.psum((jnp.sum(grad_out, axis=0), jnp.sum(grad_out * normed, axis=0)),...  75.6 us
    psum x1, waiting for transfers between devices, local(): summed = lax.psum((local_grads[0], local_grads[1], local_grads[2]), 'bins')  39 us
    unnamed x2, blocking collectives  33.9 us
    all_gather x1, blocking collectives, local(): lax.all_gather(point_weight.astype(bf), ('batch', 'fsdp'), axis=0, tiled=...  15.8 us
    dot_general x2, matrix products, contract_rows(): lax.dot_general(left, right, (((0,), (0,)), ((), ())), preferred_element_...  12.3 us
    psum x1, blocking collectives, local(): summed = lax.psum((local_grads[0], local_grads[1], local_grads[2]), 'bins')  10.6 us
  transfers between devices with their start and end apart: 8, of which 1 were waited for; matrix products, arithmetic and copies ran while one was open for 17% of the time, Pallas kernels for 0%

commit v1 on v0

--- a/solution.py
+++ b/solution.py
@@ -5,6 +5,11 @@
 
 DILATION_STEP = 26
 norm_eps = 1e-05
+
+
+def axis_by_axis(value, axis_one, axis_two):
+    half = lax.psum(value, axis_one)
+    return lax.psum(half, axis_two)
 
 
 def extended(block, sides, width):
@@ -42,8 +47,8 @@
 
 
 def norm_back(grad_out, normed, scale, gain, valid, count):
-    total, cross = lax.psum(
-        (jnp.sum(grad_out, axis=0), jnp.sum(grad_out * normed, axis=0)), ("bins", "batch", "fsdp")
+    total, cross = axis_by_axis(
+        (jnp.sum(grad_out, axis=0), jnp.sum(grad_out * normed, axis=0)), ("batch", "fsdp"), "bins"
     )
     grad_in = scale * gain * (grad_out - valid * (total + normed * cross) / count)
     return (grad_in, total, cross)

time: 468 us -> 421 us (0.90)
  blocking collectives: 297 us -> 255 us
    psum x3 -> x4, blocking collectives: 86.2 us -> 58.8 us  [the longest x2 39.9 us: axis_by_axis(): half = lax.psum(value, axis_one)]
    unnamed x2 -> x1, blocking collectives: 33.9 us -> 19.1 us
  transfers between devices with their start and end apart: 8 -> 8, of which waited for: 1 -> 1; matrix products, arithmetic and copies ran while one was open for 17% -> 18% of each run, Pallas kernels for 0% -> 0%
where the time goes in v1:
time: 421 us; the launch traced here: 420 us
  blocking collectives  255 us (61%)
  other arithmetic  42.9 us (10%)
  matrix products  42.7 us (10%)
  waiting for transfers between devices  35.4 us (8%)
  local copies, waits for them, and re-layouts  16.4 us (4%)
  between operations  16.2 us (4%)
  starting transfers between devices  11.7 us (3%)
    psum x2, blocking collectives, moments(): lax.psum(jnp.sum(centred * centred * valid, axis=0), ('bins', 'batch', 'f...  83.3 us
    psum x2, blocking collectives, moments(): lax.psum((jnp.sum(values * valid, axis=0), local_count), ('bins', 'batch'...  77.7 us
    psum x2, blocking collectives, axis_by_axis(): half = lax.psum(value, axis_one)  39.9 us
    psum x1, waiting for transfers between devices, local(): summed = lax.psum((local_grads[0], local_grads[1], local_grads[2]), 'bins')  35.4 us
    unnamed x1, blocking collectives  19.1 us
    psum x2, blocking collectives, axis_by_axis(): return lax.psum(half, axis_two)  18.9 us
    all_gather x1, blocking collectives, local(): lax.all_gather(point_weight.astype(bf), ('batch', 'fsdp'), axis=0, tiled=...  15.9 us
    dot_general x2, matrix products, contract_rows(): lax.dot_general(left, right, (((0,), (0,)), ((), ())), preferred_element_...  12.3 us
  transfers between devices with their start and end apart: 8, of which 1 were waited for; matrix products, arithmetic and copies ran while one was open for 18% of the time, Pallas kernels for 0%

profile of v1, /device:TPU:0, one launch (start us, length us, event | category | flops | bytes accessed | tf_op | source)
XLA Modules:
  0.0 420.2 jit_solution(12789915955542045329)
XLA Ops:
  7.2 1.9 convert_element_type.96
  17.5 19.1 %all-reduce.12 = (bf16[768]{0:T(1024)(128)(2,1)S(1)}, bf16[768]{0:T(1024)(128)(2,1)S(1)}, bf16[768]{0:T(1024)(128)(2,1)S(1)}, bf16[384]{0:T(512)(128)(2,1)S(1)}, bf16[384]{0:T(512)(128)(2,1)S(1)}) all-reduce(bf16[768]{0:T(1024)(128)(2,1)S(1)} %dynamic-update-slice.4, ...), channel_id=1, replica_groups=mesh['bins'=4,'batch'=4,'fsdp'=2] {'batch','fsdp'}, use_global_device_ids=true, to_apply=%add.4 | all-reduce | flops 3072 | bytes 12288
  36.7 2.6 fusion.13
  39.3 38.0 %all-reduce.6 = (f32[768]{0:T(1024)S(1)}, f32[]{:T(128)}) all-reduce(f32[768]{0:T(1024)S(1)} %fusion.13, f32[]{:T(128)} %convert_reduce_fusion.1), channel_id=1, replica_groups=mesh['bins'=4,'batch'=4,'fsdp'=2] {'bins','batch','fsdp'}, use_global_device_ids=true, to_apply=%region_1.0 | all-reduce | flops 769 | bytes 6152 | tf_op jit(solution)/shard_map/psum | solution.py:38
  79.0 41.6 %psum.117 = f32[768]{0:T(1024)S(1)} all-reduce(f32[768]{0:T(1024)S(1)} %fusion.3), channel_id=1, replica_groups=mesh['bins'=4,'batch'=4,'fsdp'=2] {'bins','batch','fsdp'}, use_global_device_ids=true, to_apply=%region_5.0 | all-reduce | flops 768 | bytes 6144 | tf_op jit(solution)/shard_map/psum | solution.py:43
  121.9 2.4 fusion.12
  124.4 4.2 %collective-permute-start = (bf16[8,26,768]{2,1,0:T(8,128)(2,1)S(1)}, bf16[8,26,768]{2,1,0:T(8,128)(2,1)S(1)}, u32[]{:S(2)}, u32[]{:S(2)}) collective-permute-start(bf16[8,26,768]{2,1,0:T(8,128)(2,1)S(1)} %get-tuple-element.40), channel_id=1, source_target_pairs={{0,8},{8,16},{16,24},{1,9},{9,17},{17,25},{2,10},{10,18},{18,26},{... | collective-permute-start | bytes 958472 | tf_op jit(solution)/shard_map/ppermute | solution.py:20
  130.0 2.3 bitcast_multiply_fusion
  132.3 15.9 %all_gather.26 = bf16[384,768]{1,0:T(8,128)(2,1)} all-gather(bf16[48,768]{1,0:T(8,128)(2,1)S(1)} %convert_element_type.102), channel_id=1, replica_groups=mesh['bins'=4,'batch'=4,'fsdp'=2] {'batch','fsdp'}, dimensions={0}, use_global_device_ids=true | all-gather | bytes 663552 | tf_op jit(solution)/shard_map/all_gather | solution.py:82
  148.2 3.6 pad_maximum_fusion.4
  151.8 9.3 %multiply_reduce_fusion.2 = (f32[384]{0:T(512)S(1)}, f32[2048,384]{1,0:T(8,128)}) fusion(f32[2048]{0:T(1024)S(1)} %bitcast.82, bf16[2304,384]{1,0:T(8,128)(2,1)} %all-gather.2.cloned.1.call-done, bf16[2048,768]{1,0:T(8,128)(2,1)} %bitcast.75, bf16[2048,768]{1,0:T(8,128)(2,1)} %bitcast.69, bf16[2048,768]{1,0:T(8,128)(2,1)} %bitcast.73), kind=kOutput, calls=%fused_computation.55 | convolution fusion | flops 3653762560 | bytes 14362112 | tf_op jit(solution)/shard_map/dot_general | solution.py:123
  161.1 39.6 %psum.118 = f32[384]{0:T(512)S(1)} all-reduce(f32[384]{0:T(512)S(1)} %get-tuple-element.51), channel_id=1, replica_groups=mesh['bins'=4,'batch'=4,'fsdp'=2] {'bins','batch','fsdp'}, use_global_device_ids=true, to_apply=%region_7.0 | all-reduce | flops 384 | bytes 3072 | tf_op jit(solution)/shard_map/psum | solution.py:38
  201.4 2.3 multiply_reduce_fusion.1
  203.8 41.7 %psum.119 = f32[384]{0:T(512)S(1)} all-reduce(f32[384]{0:T(512)S(1)} %multiply_reduce_fusion.1), channel_id=1, replica_groups=mesh['bins'=4,'batch'=4,'fsdp'=2] {'bins','batch','fsdp'}, use_global_device_ids=true, to_apply=%region_9.0 | all-reduce | flops 384 | bytes 3072 | tf_op jit(solution)/shard_map/psum | solution.py:43
  246.1 5.5 %fusion.43 = f32[384,768]{1,0:T(8,128)} fusion(bf16[2048,768]{1,0:T(8,128)(2,1)} %bitcast_multiply_fusion, f32[2048,384]{1,0:T(8,128)} %get-tuple-element.52, f32[384]{0:T(512)S(1)} %convert_element_type.100, f32[384]{0:T(512)S(1)} %convert_element_type.98, f32[384]{0:T(512)S(1)} %get-tuple-element.37, f32[384]{0:T(512)S(1)} %broadcast_divide_fusion.1), kind=kOutput, calls=%fused_computation.73 | convolution fusion | flops 1215823872 | bytes 7477248 | tf_op jit(solution)/shard_map/dot_general | solution.py:58
  251.7 7.8 %fusion.45 = (f32[384]{0:T(512)S(1)}, f32[384]{0:T(512)S(1)}, f32[2048,384]{1,0:T(8,128)}) fusion(f32[384]{0:T(512)S(1)} %get-tuple-element.37, f32[2048,384]{1,0:T(8,128)} %get-tuple-element.52, f32[384]{0:T(512)S(1)} %broadcast_divide_fusion.1, f32[384]{0:T(512)S(1)} %convert_element_type.100, f32[384]{0:T(512)S(1)} %convert_element_type.98, ...), kind=kOutput, calls=%fused_computation.75 | convolution fusion | flops 1220541696 | bytes 10036224 | tf_op jit(solution)/shard_map/dot_general | solution.py:136
  259.5 14.0 %all-reduce.8 = (f32[384]{0:T(512)S(1)}, f32[384]{0:T(512)S(1)}) all-reduce(f32[384]{0:T(512)S(1)} %get-tuple-element.12, f32[384]{0:T(512)S(1)} %get-tuple-element.11), channel_id=1, replica_groups=mesh['bins'=4,'batch'=4,'fsdp'=2] {'batch','fsdp'}, use_global_device_ids=true, to_apply=%region_14.0 | all-reduce | flops 768 | bytes 6144 | tf_op jit(solution)/shard_map/psum | solution.py:11
  273.5 9.8 %all-reduce.10 = (f32[384]{0:T(512)S(1)}, f32[384]{0:T(512)S(1)}) all-reduce(f32[384]{0:T(512)S(1)} %get-tuple-element.18, f32[384]{0:T(512)S(1)} %get-tuple-element.19), channel_id=1, replica_groups=mesh['bins'=4,'batch'=4,'fsdp'=2] {'bins'}, use_global_device_ids=true, to_apply=%region_15.0 | all-reduce | flops 768 | bytes 6144 | tf_op jit(solution)/shard_map/psum | solution.py:12
  283.3 4.5 %multiply_convert_fusion = bf16[2048,384]{1,0:T(8,128)(2,1)S(1)} fusion(f32[2048,384]{1,0:T(8,128)} %get-tuple-element.53, f32[2048,384]{1,0:T(8,128)} %get-tuple-element.52, f32[]{:T(128)} %get-tuple-element.14, f32[384]{0:T(512)S(1)} %get-tuple-element.23, f32[384]{0:T(512)S(1)} %get-tuple-element.24, f32[384]{0:T(512)S(1)} %get-tuple-element.36, ...), kind=kLoop, calls=%fused_computation.48 | loop fusion | flops 7077888 | bytes 7880196 | tf_op jit(solution)/shard_map/convert_element_type | solution.py:142
  289.0 6.8 %fusion.36 = f32[2304,384]{1,0:T(8,128)} fusion(bf16[2048,384]{1,0:T(8,128)(2,1)S(1)} %multiply_convert_fusion, bf16[2048,768]{1,0:T(8,128)(2,1)} %bitcast.76, bf16[2048,768]{1,0:T(8,128)(2,1)S(1)} %bitcast.70, bf16[2048,768]{1,0:T(8,128)(2,1)S(1)} %bitcast.74), kind=kOutput, calls=%fused_computation.43 | convolution fusion | flops 3652190208 | bytes 14548992 | tf_op jit(solution)/shard_map/dot_general | solution.py:58
  297.2 3.6 convert_reduce_fusion
  300.8 1.8 fusion.48
  303.9 4.8 %collective-permute-start.3 = (bf16[8,26,384]{2,1,0:T(8,128)(2,1)}, bf16[8,26,384]{2,1,0:T(8,128)(2,1)S(1)}, u32[]{:S(2)}, u32[]{:S(2)}) collective-permute-start(bf16[8,26,384]{2,1,0:T(8,128)(2,1)} %get-tuple-element.45), channel_id=1, source_target_pairs={{0,8},{8,16},{16,24},{1,9},{9,17},{17,25},{2,10},{10,18},{18,26},{... | collective-permute-start | bytes 479240 | tf_op jit(solution)/shard_map/ppermute | solution.py:20
  308.7 4.9 %fusion.15 = bf16[2048,768]{1,0:T(8,128)(2,1)} fusion(bf16[8,256,768]{2,1,0:T(8,128)(2,1)S(1)} %copy-done, bf16[384,768]{1,0:T(8,128)(2,1)S(1)} %copy-done.9, f32[768]{0:T(1024)S(1)} %copy-done.21, f32[2048,384]{1,0:T(8,128)S(1)} %copy-done.4, f32[384]{0:T(512)} %copy-done.25, f32[384]{0:T(512)} %copy-done.24, f32[384]{0:T(512)} %copy-done.20, ...), kind=kOutput, calls=%fused_computation.20 | convolution fusion | flops 1222115328 | bytes 10036224 | tf_op jit(solution)/shard_map/dot_general | solution.py:127
  316.1 3.9 copy.22
  320.0 3.1 pad_maximum_fusion.6
  323.2 8.4 %fusion.44 = (f32[768]{0:T(1024)S(1)}, f32[768]{0:T(1024)S(1)}, f32[2048,768]{1,0:T(8,128)}) fusion(f32[768]{0:T(1024)S(1)} %get-tuple-element.33, f32[768]{0:T(1024)S(1)} %broadcast_divide_fusion, bf16[8,256,768]{2,1,0:T(8,128)(2,1)S(1)} %copy-done, f32[768]{0:T(1024)S(1)} %copy-done.18, f32[768]{0:T(1024)S(1)} %copy-done.16, ...), kind=kOutput, calls=%fused_computation.74 | convolution fusion | flops 3664771584 | bytes 15943680 | tf_op jit(solution)/shard_map/dot_general | solution.py:164
  331.5 25.9 %all-reduce.7 = (f32[768]{0:T(1024)S(1)}, f32[768]{0:T(1024)S(1)}, f32[768]{0:T(1024)S(1)}) all-reduce(f32[768]{0:T(1024)S(1)} %get-tuple-element.10, f32[768]{0:T(1024)S(1)} %get-tuple-element.9, f32[768]{0:T(1024)S(1)} %copy-done.14), channel_id=1, replica_groups=mesh['bins'=4,'batch'=4,'fsdp'=2] {'batch','fsdp'}, use_global_device_ids=true, to_apply=%region_20.0 | all-reduce | flops 2304 | bytes 18432 | tf_op jit(solution)/shard_map/psum | solution.py:11
  357.5 9.1 %all-reduce.9 = (f32[768]{0:T(1024)S(1)}, f32[768]{0:T(1024)S(1)}, f32[96]{0:T(128)}) all-reduce(f32[768]{0:T(1024)S(1)} %get-tuple-element.15, f32[768]{0:T(1024)S(1)} %get-tuple-element.16, f32[96]{0:T(128)S(1)} %dynamic-slice.6), channel_id=1, replica_groups=mesh['bins'=4,'batch'=4,'fsdp'=2] {'bins'}, use_global_device_ids=true, to_apply=%region_21.0 | all-reduce | flops 1632 | bytes 13056 | tf_op jit(solution)/shard_map/psum | solution.py:12
  366.7 7.1 %fusion.29 = bf16[2048,768]{1,0:T(8,128)(2,1)} fusion(f32[2048,768]{1,0:T(8,128)} %get-tuple-element.54, bf16[8,256,768]{2,1,0:T(8,128)(2,1)S(1)} %copy-done, f32[]{:T(128)} %get-tuple-element.14, f32[768]{0:T(1024)S(1)} %get-tuple-element.20, f32[768]{0:T(1024)S(1)} %get-tuple-element.21, f32[2048]{0:T(1024)S(1)} %bitcast.85, ...), kind=kLoop, calls=%fused_computation.36 | loop fusion | flops 20447232 | bytes 15756292 | tf_op jit(solution)/shard_map/convert_element_type | solution.py:172
  374.9 35.4 %all-reduce.15.cloned.1.call-done = (f32[288,384]{1,0:T(8,128)}, f32[48,768]{1,0:T(8,128)}) async-done(((f32[288,384]{1,0:T(8,128)}, f32[48,768]{1,0:T(8,128)}), (f32[288,384]{1,0:T(8,128)}, f32[48,768]{1,0:T(8,128)})) %all-reduce.15.cloned.1.call-update) | async-done | bytes 589840 | tf_op jit(solution)/shard_map/psum | solution.py:176
  410.2 1.8 copy.32
  (109 shorter events, 21.4 us)
Async XLA Ops:
  7.2 70.8 %copy-start = (bf16[8,256,768]{2,1,0:T(8,128)(2,1)S(1)}, bf16[8,256,768]{2,1,0:T(8,128)(2,1)}, u32[]{:S(2)}) copy-start(bf16[8,256,768]{2,1,0:T(8,128)(2,1)} %param.12) | copy-start | bytes 9437188
  7.2 144.6 %all-gather.2.cloned.1.call-start = ((), (), s32[]{:S(2)}) async-start(), calls=%async_computation.2 | async-start | bytes 1990656 | tf_op jit(solution)/shard_map/all_gather | solution.py:81
  9.1 357.5 %reduce-scatter.5.cloned.1.call-start = ((), (), s32[]{:S(2)}) async-start(), calls=%async_computation.4 | async-start | bytes 1327104 | tf_op jit(solution)/shard_map/reduce_scatter | solution.py:179
  36.6 85.2 %copy-start.15 = (f32[768]{0:T(1024)}, f32[768]{0:T(1024)S(1)}, u32[]{:S(2)}) copy-start(f32[768]{0:T(1024)S(1)} %convert_element_type.92) | copy-start | bytes 9220
  36.7 85.2 %copy-start.17 = (f32[768]{0:T(1024)}, f32[768]{0:T(1024)S(1)}, u32[]{:S(2)}) copy-start(f32[768]{0:T(1024)S(1)} %convert_element_type.94) | copy-start | bytes 9220
  121.9 8.1 %copy-start.1 = (bf16[8,256,768]{2,1,0:T(8,128)(2,1)S(1)}, bf16[8,256,768]{2,1,0:T(8,128)(2,1)}, u32[]{:S(2)}) copy-start(bf16[8,256,768]{2,1,0:T(8,128)(2,1)} %param.23) | copy-start | bytes 9437188
  124.3 23.9 %copy-start.2 = (bf16[8,256,768]{2,1,0:T(8,128)(2,1)}, bf16[8,256,768]{2,1,0:T(8,128)(2,1)S(1)}, u32[]{:S(2)}) copy-start(bf16[8,256,768]{2,1,0:T(8,128)(2,1)S(1)} %fusion.12) | copy-start | bytes 9437188
  124.4 23.8 %collective-permute-start = (bf16[8,26,768]{2,1,0:T(8,128)(2,1)S(1)}, bf16[8,26,768]{2,1,0:T(8,128)(2,1)S(1)}, u32[]{:S(2)}, u32[]{:S(2)}) collective-permute-start(bf16[8,26,768]{2,1,0:T(8,128)(2,1)S(1)} %get-tuple-element.40), channel_id=1, source_target_pairs={{0,8},{8,16},{16,24},{1,9},{9,17},{17,25},{2,10},{10,18},{18,26},{... | collective-permute-start | bytes 958472 | tf_op jit(solution)/shard_map/ppermute | solution.py:20
  128.6 19.6 %collective-permute-start.1 = (bf16[8,26,768]{2,1,0:T(8,128)(2,1)S(1)}, bf16[8,26,768]{2,1,0:T(8,128)(2,1)S(1)}, u32[]{:S(2)}, u32[]{:S(2)}) collective-permute-start(bf16[8,26,768]{2,1,0:T(8,128)(2,1)S(1)} %get-tuple-element.41), channel_id=1, source_target_pairs={{8,0},{16,8},{24,16},{9,1},{17,9},{25,17},{10,2},{18,10},{26,18},{... | collective-permute-start | bytes 958472 | tf_op jit(solution)/shard_map/ppermute | solution.py:23
  130.0 2.3 copy-start.10
  132.3 119.4 %copy-start.24 = (f32[384]{0:T(512)}, f32[384]{0:T(512)S(1)}, u32[]{:S(2)}) copy-start(f32[384]{0:T(512)S(1)} %convert_element_type.98) | copy-start | bytes 4612
  132.3 119.4 %copy-start.25 = (f32[384]{0:T(512)}, f32[384]{0:T(512)S(1)}, u32[]{:S(2)}) copy-start(f32[384]{0:T(512)S(1)} %convert_element_type.100) | copy-start | bytes 4612
  201.4 81.9 %copy-start.13 = (f32[384]{0:T(512)}, f32[384]{0:T(512)S(1)}, u32[]{:S(2)}) copy-start(f32[384]{0:T(512)S(1)} %broadcast_divide_fusion.1) | copy-start | bytes 4612
  246.1 37.2 %copy-start.20 = (f32[384]{0:T(512)}, f32[384]{0:T(512)S(1)}, u32[]{:S(2)}) copy-start(f32[384]{0:T(512)S(1)} %get-tuple-element.37) | copy-start | bytes 4612
  251.6 115.0 %reduce-scatter.3.cloned.1.call-start = ((), (), s32[]{:S(2)}) async-start(), calls=%async_computation.3 | async-start | bytes 3981312 | tf_op jit(solution)/shard_map/reduce_scatter | solution.py:178
  283.3 4.6 %copy-start.22 = (f32[384]{0:T(512)}, f32[384]{0:T(512)S(1)}, u32[]{:S(2)}) copy-start(f32[384]{0:T(512)S(1)} %get-tuple-element.24) | copy-start | bytes 4612
  283.3 4.6 %copy-start.23 = (f32[384]{0:T(512)}, f32[384]{0:T(512)S(1)}, u32[]{:S(2)}) copy-start(f32[384]{0:T(512)S(1)} %get-tuple-element.23) | copy-start | bytes 4612
  283.3 5.7 %copy-start.3 = (bf16[8,256,768]{2,1,0:T(8,128)(2,1)S(1)}, bf16[8,256,768]{2,1,0:T(8,128)(2,1)}, u32[]{:S(2)}) copy-start(bf16[8,256,768]{2,1,0:T(8,128)(2,1)} %copy-done.2) | copy-start | bytes 9437188
  283.3 5.7 %copy-start.7 = (bf16[8,256,768]{2,1,0:T(8,128)(2,1)S(1)}, bf16[8,256,768]{2,1,0:T(8,128)(2,1)}, u32[]{:S(2)}) copy-start(bf16[8,256,768]{2,1,0:T(8,128)(2,1)} %get-tuple-element.38) | copy-start | bytes 9437188
  295.8 114.4 %all-reduce.15.cloned.1.call-start = ((), (), s32[]{:S(2)}) async-start(), calls=%async_computation.5 | async-start | bytes 1179648 | tf_op jit(solution)/shard_map/psum | solution.py:176
  297.1 11.5 %copy-start.4 = (f32[2048,384]{1,0:T(8,128)S(1)}, f32[2048,384]{1,0:T(8,128)}, u32[]{:S(2)}) copy-start(f32[2048,384]{1,0:T(8,128)} %get-tuple-element.52) | copy-start | bytes 9437188
  297.1 11.5 %copy-start.9 = (bf16[384,768]{1,0:T(8,128)(2,1)S(1)}, bf16[384,768]{1,0:T(8,128)(2,1)}, u32[]{:S(2)}) copy-start(bf16[384,768]{1,0:T(8,128)(2,1)} %all_gather.26) | copy-start | bytes 1769476
  297.1 11.5 %copy-start.21 = (f32[768]{0:T(1024)S(1)}, f32[768]{0:T(1024)}, u32[]{:S(2)}) copy-start(f32[768]{0:T(1024)} %convert_element_type.104) | copy-start | bytes 9220
  302.6 17.4 %collective-permute-start.2 = (bf16[8,26,384]{2,1,0:T(8,128)(2,1)}, bf16[8,26,384]{2,1,0:T(8,128)(2,1)S(1)}, u32[]{:S(2)}, u32[]{:S(2)}) collective-permute-start(bf16[8,26,384]{2,1,0:T(8,128)(2,1)} %get-tuple-element.44), channel_id=1, source_target_pairs={{8,0},{16,8},{24,16},{9,1},{17,9},{25,17},{10,2},{18,10},{26,18},{... | collective-permute-start | bytes 479240 | tf_op jit(solution)/shard_map/ppermute | solution.py:23
  303.9 16.1 %collective-permute-start.3 = (bf16[8,26,384]{2,1,0:T(8,128)(2,1)}, bf16[8,26,384]{2,1,0:T(8,128)(2,1)S(1)}, u32[]{:S(2)}, u32[]{:S(2)}) collective-permute-start(bf16[8,26,384]{2,1,0:T(8,128)(2,1)} %get-tuple-element.45), channel_id=1, source_target_pairs={{0,8},{8,16},{16,24},{1,9},{9,17},{17,25},{2,10},{10,18},{18,26},{... | collective-permute-start | bytes 479240 | tf_op jit(solution)/shard_map/ppermute | solution.py:20
  319.9 3.2 copy-start.6
  319.9 3.2 copy-start.8
  320.0 3.2 copy-start.16
  320.0 3.2 copy-start.18
  323.1 8.4 %copy-start.14 = (f32[768]{0:T(1024)S(1)}, f32[768]{0:T(1024)}, u32[]{:S(2)}) copy-start(f32[768]{0:T(1024)} %convert_reduce_fusion) | copy-start | bytes 9220
  323.2 43.5 %copy-start.12 = (bf16[1,2,8,128]{3,1,2,0:T(2,128)(2,1)S(1)}, bf16[1,2,8,128]{3,1,2,0:T(2,128)(2,1)}, u32[]{:S(2)}) copy-start(bf16[1,2,8,128]{3,1,2,0:T(2,128)(2,1)} %copy-done.11) | copy-start | bytes 12292
  323.2 43.5 %copy-start.19 = (f32[768]{0:T(1024)S(1)}, f32[768]{0:T(1024)}, u32[]{:S(2)}) copy-start(f32[768]{0:T(1024)} %get-tuple-element.32) | copy-start | bytes 9220
  (2 other events, 3.4 us)
Sparse Core Ops, SparseCore 0:
  10.2 29.7 all-gather.1
  251.7 32.1 reduce-scatter.4
  295.9 40.6 reduce-scatter.2
  366.8 43.4 all-reduce.14
